TPU v7x, 32 devices: a whole 2x2x4 slice. The times are simulated.
32 devices in a mesh: seq: 8 (over z, y), head: 4 (over x, core).
Axes of the slice: x: 2, y: 2, z: 4, core: 2. Of those that a mesh axis runs over, the one named last changes fastest.
Arguments:
- query: bfloat16 [4096, 8192], P('seq', 'head'), may hold values from -1.5 to 1.5
- key_in: bfloat16 [4096, 8192], P('seq', 'head'), may hold values from -0.5 to 0.5
- value: bfloat16 [4096, 8192], P('seq', 'head'), may hold values from -6 to 6
- gate: bfloat16 [4096, 8192], P(('seq', 'head')), may hold values from -6 to 6
- gain: float32 [8192], replicated, may hold values from 0.5 to 1.5
- grad_out: bfloat16 [4096, 8192], P(('seq', 'head')), may hold values from -6 to 6
Outputs:
- grad_query: bfloat16 [4096, 8192], P('seq', 'head')
- grad_key: bfloat16 [4096, 8192], P('seq', 'head')
- grad_value: bfloat16 [4096, 8192], P('seq', 'head')
- grad_gate: bfloat16 [4096, 8192], P(('seq', 'head'))
All inputs are finite; a program needn't handle non-finite values.
Results may differ from a plain program's by a relative error of at most 0.012.
Values may be sent and summed in bfloat16 or wider, within the bound.
A program may use at most 128 MiB of HBM per device.

v0:
```python
import jax
import jax.numpy as jnp
from jax import lax
from jax.sharding import PartitionSpec as P

HEAD_DIM = 128


def carried_in(value, axis, combine, identity):
    peers, place = (lax.axis_size(axis), lax.axis_index(axis))
    everything = lax.all_gather(value.astype(jnp.bfloat16), axis)
    start = jnp.broadcast_to(jnp.asarray(identity, value.dtype), value.shape)

    def step(k, before):
        at = peers - 1 - k
        reached = at > place
        new = combine(before, everything[at].astype(value.dtype))
        return jnp.where(reached, new, before)

    return lax.fori_loop(0, peers, step, start)


def add_states(earlier, later_part):
    return earlier + later_part


def split_heads(matrix, head_dim):
    return matrix.reshape(matrix.shape[0], matrix.shape[1] // head_dim, head_dim)


def on_device(query, key_in, value, gate, gain, grad_out):
    head_dim = HEAD_DIM
    tok_here = query.shape[0]
    queries = split_heads(query, head_dim)
    keys_here = split_heads(key_in, head_dim)
    values_here = split_heads(value, head_dim)
    local_state = jnp.einsum(
        "thd,the->hde", keys_here, values_here, preferred_element_type=jnp.float32
    )
    zero_state = jnp.zeros_like(local_state)
    my_index = lax.axis_index("seq")
    shard_piece = lax.all_gather(
        local_state[None].astype(jnp.bfloat16), "seq", axis=0, tiled=True
    ).astype(jnp.float32)
    position = jnp.arange(shard_piece.shape[0], dtype=jnp.int32)
    keep_rows = (position < my_index).astype(jnp.float32)
    prefix = zero_state + jnp.sum(keep_rows[:, None, None, None] * shard_piece, axis=0)
    causal = jnp.tril(jnp.ones((tok_here, tok_here), dtype=bool))
    scores = jnp.einsum("thd,shd->hts", queries, keys_here, preferred_element_type=jnp.float32)
    masked_scores = jnp.where(causal[None], scores, 0.0).astype(jnp.bfloat16)
    prefix_low = prefix.astype(jnp.bfloat16)
    attn_out = jnp.einsum(
        "hts,she->the", masked_scores, values_here, preferred_element_type=jnp.float32
    )
    attn_out = attn_out + jnp.einsum(
        "thd,hde->the", queries, prefix_low, preferred_element_type=jnp.float32
    )
    attn_out = attn_out.astype(jnp.bfloat16).reshape(tok_here, -1)
    token_rows = lax.all_to_all(attn_out, "head", split_axis=0, concat_axis=1, tiled=True)
    rows_wide = token_rows.astype(jnp.float32)
    inv_rms = lax.rsqrt(jnp.mean(rows_wide * rows_wide, axis=1, keepdims=True) + 1e-06)
    normed = rows_wide * inv_rms
    gate_wide = gate.astype(jnp.float32)
    sigmoid_gate = jax.nn.sigmoid(gate_wide)
    scaled = grad_out.astype(jnp.float32) * gain[None, :]
    grad_gate = (scaled * normed * sigmoid_gate * (1.0 + gate_wide * (1.0 - sigmoid_gate))).astype(
        jnp.bfloat16
    )
    weighted = scaled * gate_wide * sigmoid_gate
    grad_rows = inv_rms * (weighted - normed * jnp.mean(weighted * normed, axis=1, keepdims=True))
    grad_rows = grad_rows.astype(jnp.bfloat16)
    grad_heads = lax.all_to_all(grad_rows, "head", split_axis=1, concat_axis=0, tiled=True)
    grad_attn = split_heads(grad_heads, head_dim)
    local_grad = jnp.einsum("thd,the->hde", queries, grad_attn, preferred_element_type=jnp.float32)
    suffix = carried_in(local_grad, "seq", add_states, zero_state)
    suffix_low = suffix.astype(jnp.bfloat16)
    grad_scores = jnp.einsum(
        "the,she->hts", grad_attn, values_here, preferred_element_type=jnp.float32
    )
    grad_scores = jnp.where(causal[None], grad_scores, 0.0).astype(jnp.bfloat16)
    grad_query = jnp.einsum(
        "hts,shd->thd", grad_scores, keys_here, preferred_element_type=jnp.float32
    )
    grad_query = grad_query + jnp.einsum(
        "the,hde->thd", grad_attn, prefix_low, preferred_element_type=jnp.float32
    )
    grad_key = jnp.einsum("hts,thd->shd", grad_scores, queries, preferred_element_type=jnp.float32)
    grad_key = grad_key + jnp.einsum(
        "she,hde->shd", values_here, suffix_low, preferred_element_type=jnp.float32
    )
    grad_value = jnp.einsum(
        "hts,the->she", masked_scores, grad_attn, preferred_element_type=jnp.float32
    )
    grad_value = grad_value + jnp.einsum(
        "shd,hde->she", keys_here, suffix_low, preferred_element_type=jnp.float32
    )
    return (
        grad_query.astype(jnp.bfloat16).reshape(tok_here, -1),
        grad_key.astype(jnp.bfloat16).reshape(tok_here, -1),
        grad_value.astype(jnp.bfloat16).reshape(tok_here, -1),
        grad_gate,
    )


def solution(mesh):
    in_specs = (
        P("seq", "head"),
        P("seq", "head"),
        P("seq", "head"),
        P(("seq", "head"), None),
        P(),
        P(("seq", "head"), None),
    )
    out_specs = (P("seq", "head"), P("seq", "head"), P("seq", "head"), P(("seq", "head"), None))
    return jax.shard_map(
        on_device, mesh=mesh, in_specs=in_specs, out_specs=out_specs, check_vma=False
    )
```

profile of v0, /device:TPU:0, one launch (start us, length us, event | category | flops | bytes accessed | tf_op | source)
XLA Modules:
  0.0 316.0 jit_solution(6141891403211392233)
XLA Ops:
  7.2 3.7 %copy.120 = bf16[64,8,16,128]{3,2,1,0:T(8,128)(2,1)} copy(bf16[64,8,16,128]{3,1,2,0:T(8,128)(2,1)} %bitcast.129) | data formatting | bytes 4194304
  10.9 4.3 %copy.88 = bf16[512,16,128]{0,2,1:T(8,128)(2,1)} copy(bf16[512,16,128]{2,1,0:T(8,128)(2,1)} %bitcast.128) | data formatting | bytes 4194304 | tf_op jit(solution)/shard_map/reshape | solution.py:28
  15.2 3.1 fusion.39
  18.4 4.6 %select_convert_fusion.1 = bf16[16,512,512]{2,1,0:T(8,128)(2,1)S(1)} fusion(pred[512,512]{1,0:T(8,128)(4,1)S(1)} %iota_compare_fusion, bf16[512,2048]{1,0:T(8,128)(2,1)} %param.9, bf16[512,2048]{1,0:T(8,128)(2,1)} %param.8), kind=kOutput, calls=%fused_computation.2 | convolution fusion | flops 1082130432 | bytes 12845056 | tf_op jit(solution)/shard_map/thd,shd->hts/dot_general | solution.py:49
  23.1 3.2 %copy-done.1 = bf16[16,512,512]{2,1,0:T(8,128)(2,1)} copy-done((bf16[16,512,512]{2,1,0:T(8,128)(2,1)}, bf16[16,512,512]{2,1,0:T(8,128)(2,1)S(1)}, u32[]{:S(2)}) %copy-start.1) | copy-done | bytes 8388632
  26.3 4.3 %fusion.17 = f32[16,512,128]{2,1,0:T(8,128)} fusion(bf16[16,512,512]{2,1,0:T(8,128)(2,1)S(1)} %select_convert_fusion.1, bf16[512,2048]{1,0:T(8,128)(2,1)S(1)} %copy-done), kind=kOutput, calls=%fused_computation.34 | convolution fusion | flops 1073741824 | bytes 14680064 | tf_op jit(solution)/shard_map/hts,she->the/dot_general | solution.py:52
  30.6 63.4 %all-gather.5.cloned.1.call-done = bf16[128,128,128]{2,1,0:T(8,128)(2,1)} async-done(((bf16[16,128,128]{2,1,0:T(8,128)(2,1)}), bf16[128,128,128]{2,1,0:T(8,128)(2,1)}) %all-gather.5.cloned.1.call-update) | async-done | bytes 4194320 | tf_op jit(solution)/shard_map/all_gather | solution.py:42
  94.0 3.3 %fusion = bf16[16,128,128]{2,1,0:T(8,128)(2,1)S(1)} fusion(bf16[8,16,128,128]{3,2,1,0:T(8,128)(2,1)} %bitcast.132, f32[8]{0:T(128)S(1)} %compare_convert_fusion), kind=kLoop, calls=%fused_computation.4 | loop fusion | flops 6029312 | bytes 4718624 | tf_op jit(solution)/shard_map/reduce_sum | solution.py:47
  102.6 4.2 %all_to_all.22 = bf16[4,128,2048]{2,1,0:T(8,128)(2,1)} reshape(bf16[512,16,128]{2,1,0:T(8,128)(2,1)} %copy.93) | data formatting | bytes 4194304 | tf_op jit(solution)/shard_map/all_to_all | solution.py:59
  106.8 4.5 %all-to-all-start = ((bf16[4,128,2048]{2,1,0:T(8,128)(2,1)}), bf16[4,128,2048]{2,1,0:T(8,128)(2,1)}, u32[]{:S(2)}, u32[]{:S(2)}) async-start(bf16[4,128,2048]{2,1,0:T(8,128)(2,1)} %all_to_all.22), calls=%async_computation | async-start | bytes 4194304 | tf_op jit(solution)/shard_map/all_to_all | solution.py:59
  111.5 4.1 %copy.95 = bf16[128,8192]{0,1:T(8,128)(2,1)} copy(bf16[128,8192]{1,0:T(8,128)(2,1)} %param.11) | data formatting | bytes 4194304 | tf_op args[3]
  115.5 4.1 %copy.94 = bf16[128,8192]{0,1:T(8,128)(2,1)} copy(bf16[128,8192]{1,0:T(8,128)(2,1)} %param.13) | data formatting | bytes 4194304 | tf_op args[5]
  119.6 17.4 %all-to-all-done = bf16[4,128,2048]{2,1,0:T(8,128)(2,1)} async-done(((bf16[4,128,2048]{2,1,0:T(8,128)(2,1)}), bf16[4,128,2048]{2,1,0:T(8,128)(2,1)}, u32[]{:S(2)}, u32[]{:S(2)}) %all-to-all-start) | async-done | bytes 2097184 | tf_op jit(solution)/shard_map/all_to_all | solution.py:59
  139.0 4.1 %convert_bitcast_fusion = f32[128,4,2048]{2,0,1:T(8,128)} fusion(bf16[4,128,2048]{2,1,0:T(8,128)(2,1)} %all-to-all-done), kind=kLoop, calls=%fused_computation.8 | loop fusion | flops 1048576 | bytes 6291456 | tf_op jit(solution)/shard_map/convert_element_type | solution.py:60
  143.1 5.4 %copy.96 = f32[128,4,2048]{0,2,1:T(8,128)} copy(f32[128,4,2048]{2,0,1:T(8,128)} %convert_bitcast_fusion) | data formatting | bytes 8388608 | tf_op jit(solution)/shard_map/convert_element_type | solution.py:60
  148.5 6.7 %multiply_reduce_fusion = f32[128]{0:T(128)S(1)} fusion(f32[128,4,2048]{0,2,1:T(8,128)} %copy.96, f32[128]{0:T(128)S(1)} %add_rsqrt_fusion, bf16[128,8192]{0,1:T(8,128)(2,1)} %copy.95, f32[8192]{0:T(1024)S(1)} %copy-done.12, bf16[128,8192]{0,1:T(8,128)(2,1)} %copy.94), kind=kLoop, calls=%fused_computation.27 | loop fusion | flops 11534208 | bytes 8422400 | tf_op jit(solution)/shard_map/reduce_sum | solution.py:70
  155.3 4.4 %fusion.8 = (bf16[128,8192]{0,1:T(8,128)(2,1)}, bf16[128,8192]{0,1:T(8,128)(2,1)}) fusion(bf16[128,8192]{0,1:T(8,128)(2,1)S(1)} %copy-done.6, bf16[128,8192]{0,1:T(8,128)(2,1)S(1)} %copy-done.7, f32[128,4,2048]{0,2,1:T(8,128)S(1)} %copy-done.2, f32[8192]{0:T(1024)S(1)} %copy-done.12, f32[128]{0:T(128)S(1)} %add_rsqrt_fusion, f32[128]{0:T(128)S(1)} %broadcast_multiply_fusion), kind=kLoop, calls=%fused_computation.17 | loop fusion | flops 20971520 | bytes 12616704 | tf_op jit(solution)/shard_map/convert_element_type | solution.py:66
  159.7 3.9 %copy.97 = bf16[128,4,2048]{2,0,1:T(8,128)(2,1)} copy(bf16[128,4,2048]{0,2,1:T(8,128)(2,1)} %bitcast.124) | data formatting | bytes 4194304 | tf_op jit(solution)/shard_map/all_to_all | solution.py:72
  163.7 29.2 %all_to_all.29 = bf16[128,4,2048]{2,0,1:T(8,128)(2,1)S(1)} all-to-all(bf16[128,4,2048]{2,0,1:T(8,128)(2,1)} %copy.97), channel_id=1, replica_groups=mesh['seq'=8,'head'=4] {'head'}, dimensions={1} | all-to-all | bytes 4194304 | tf_op jit(solution)/shard_map/all_to_all | solution.py:72
  194.9 4.3 %copy.103 = bf16[512,16,128]{0,2,1:T(8,128)(2,1)} copy(bf16[512,16,128]{2,1,0:T(8,128)(2,1)} %bitcast.127) | data formatting | bytes 4194304 | tf_op jit(solution)/shard_map/reshape | solution.py:28
  199.2 2.9 fusion.42
  203.2 4.1 %copy.113 = bf16[128,8192]{1,0:T(8,128)(2,1)} copy(bf16[128,8192]{0,1:T(8,128)(2,1)} %get-tuple-element.166) | data formatting | bytes 4194304
  207.3 4.4 %select_convert_fusion = bf16[16,512,512]{2,1,0:T(8,128)(2,1)S(1)} fusion(bf16[512,16,128]{0,2,1:T(8,128)(2,1)} %copy.103, pred[512,512]{1,0:T(8,128)(4,1)S(1)} %iota_compare_fusion, bf16[512,2048]{1,0:T(8,128)(2,1)S(1)} %copy-done), kind=kOutput, calls=%fused_computation.1 | convolution fusion | flops 1082130432 | bytes 12845056 | tf_op jit(solution)/shard_map/the,she->hts/dot_general | solution.py:77
  211.7 4.8 %fusion.49 = f32[16,512,128]{1,2,0:T(8,128)} fusion(bf16[16,512,512]{2,1,0:T(8,128)(2,1)S(1)} %select_convert_fusion, bf16[512,16,128]{0,2,1:T(8,128)(2,1)S(1)} %copy-done.9), kind=kOutput, calls=%fused_computation.64 | convolution fusion | flops 1073741824 | bytes 14680064 | tf_op jit(solution)/shard_map/hts,shd->thd/dot_general | solution.py:81
  216.5 4.5 %fusion.10 = bf16[512,16,128]{0,2,1:T(8,128)(2,1)} fusion(f32[16,512,128]{1,2,0:T(8,128)} %fusion.49, bf16[512,16,128]{0,2,1:T(8,128)(2,1)S(1)} %copy-done.5, bf16[16,128,128]{2,1,0:T(8,128)(2,1)} %copy-done.11), kind=kOutput, calls=%fused_computation.21 | convolution fusion | flops 270532608 | bytes 8912896 | tf_op jit(solution)/shard_map/the,hde->thd/dot_general | solution.py:84
  221.0 3.9 %copy.110 = bf16[512,2048]{1,0:T(8,128)(2,1)} copy(bf16[512,2048]{0,1:T(8,128)(2,1)} %bitcast.125) | data formatting | bytes 4194304
  224.9 7.3 %fusion.50 = f32[16,128,512]{2,1,0:T(8,128)} fusion(bf16[512,16,128]{0,2,1:T(8,128)(2,1)} %copy.103, bf16[16,512,512]{2,1,0:T(8,128)(2,1)} %copy-done.1), kind=kOutput, calls=%fused_computation.65 | convolution fusion | flops 1073741824 | bytes 14680064 | tf_op jit(solution)/shard_map/hts,the->she/dot_general | solution.py:91
  232.2 41.6 %all-gather.7.cloned.1.call-done = bf16[128,128,128]{2,1,0:T(8,128)(2,1)} async-done(((bf16[16,128,128]{2,1,0:T(8,128)(2,1)}), bf16[128,128,128]{2,1,0:T(8,128)(2,1)}) %all-gather.7.cloned.1.call-update) | async-done | bytes 4194320 | tf_op jit(solution)/shard_map/all_gather | solution.py:11
  273.8 13.1 %while.16 = (s32[]{:T(128)}, f32[16,128,128]{2,1,0:T(8,128)S(1)}, s32[]{:T(128)}, bf16[8,16,128,128]{3,2,1,0:T(8,128)(2,1)}, s32[]{:T(128)}, /*index=5*/s32[]{:T(128)}, s32[]{:T(128)}, s32[]{:T(128)}) while((s32[]{:T(128)}, f32[16,128,128]{2,1,0:T(8,128)S(1)}, s32[]{:T(128)}, bf16[8,16,128,128]{3,2,1,0:T(8,128)(2,1)}, s32[]{:T(128)}, ...), condition=%wide.region_4.5_spmd.clone, body=%wide.region_3.4_spmd.clone.sunk | while | flops 1048584 | bytes 2621603 | solution.py:20
  293.4 3.9 %copy.112 = bf16[512,2048]{1,0:T(8,128)(2,1)} copy(bf16[512,2048]{0,1:T(8,128)(2,1)} %bitcast.130) | data formatting | bytes 4194304
  297.3 7.9 %fusion.9 = bf16[512,16,128]{0,2,1:T(8,128)(2,1)} fusion(f32[16,128,512]{2,1,0:T(8,128)} %fusion.12, bf16[16,512,512]{2,1,0:T(8,128)(2,1)} %copy-done.3, bf16[512,2048]{1,0:T(8,128)(2,1)} %param.8), kind=kOutput, calls=%fused_computation.19 | convolution fusion | flops 1075838976 | bytes 16777216 | tf_op jit(solution)/shard_map/hts,thd->shd/dot_general | solution.py:87
  305.3 3.9 %copy.111 = bf16[512,2048]{1,0:T(8,128)(2,1)} copy(bf16[512,2048]{0,1:T(8,128)(2,1)} %bitcast.131) | data formatting | bytes 4194304
  (49 shorter events, 30.3 us)
Async XLA Ops:
  7.2 8.0 %copy-start = (bf16[512,2048]{1,0:T(8,128)(2,1)S(1)}, bf16[512,2048]{1,0:T(8,128)(2,1)}, u32[]{:S(2)}) copy-start(bf16[512,2048]{1,0:T(8,128)(2,1)} %param.10) | copy-start | bytes 6291460
  7.2 86.8 %all-gather.5.cloned.1.call-start = ((), (), s32[]{:S(2)}) async-start(), calls=%async_computation.2 | async-start | bytes 4718592 | tf_op jit(solution)/shard_map/all_gather | solution.py:42
  23.0 3.2 %copy-start.1 = (bf16[16,512,512]{2,1,0:T(8,128)(2,1)}, bf16[16,512,512]{2,1,0:T(8,128)(2,1)S(1)}, u32[]{:S(2)}) copy-start(bf16[16,512,512]{2,1,0:T(8,128)(2,1)S(1)} %select_convert_fusion.1) | copy-start | bytes 25165828
  94.0 3.4 %copy-start.8 = (f32[16,512,128]{2,1,0:T(8,128)S(1)}, f32[16,512,128]{2,1,0:T(8,128)}, u32[]{:S(2)}) copy-start(f32[16,512,128]{2,1,0:T(8,128)} %fusion.17) | copy-start | bytes 12582916
  97.4 2.5 copy-start.11
  106.8 30.2 %all-to-all-start = ((bf16[4,128,2048]{2,1,0:T(8,128)(2,1)}), bf16[4,128,2048]{2,1,0:T(8,128)(2,1)}, u32[]{:S(2)}, u32[]{:S(2)}) async-start(bf16[4,128,2048]{2,1,0:T(8,128)(2,1)} %all_to_all.22), calls=%async_computation | async-start | bytes 4194304 | tf_op jit(solution)/shard_map/all_to_all | solution.py:59
  111.2 162.5 %all-gather.7.cloned.1.call-start = ((), (), s32[]{:S(2)}) async-start(), calls=%async_computation.3 | async-start | bytes 4718592 | tf_op jit(solution)/shard_map/all_gather | solution.py:11
  143.1 5.4 %copy-start.12 = (f32[8192]{0:T(1024)S(1)}, f32[8192]{0:T(1024)}, u32[]{:S(2)}) copy-start(f32[8192]{0:T(1024)} %param.12) | copy-start | bytes 98308
  148.5 6.8 %copy-start.2 = (f32[128,4,2048]{0,2,1:T(8,128)S(1)}, f32[128,4,2048]{0,2,1:T(8,128)}, u32[]{:S(2)}) copy-start(f32[128,4,2048]{0,2,1:T(8,128)} %copy.96) | copy-start | bytes 12582916
  148.5 6.8 %copy-start.6 = (bf16[128,8192]{0,1:T(8,128)(2,1)S(1)}, bf16[128,8192]{0,1:T(8,128)(2,1)}, u32[]{:S(2)}) copy-start(bf16[128,8192]{0,1:T(8,128)(2,1)} %copy.95) | copy-start | bytes 6291460
  148.5 6.8 %copy-start.7 = (bf16[128,8192]{0,1:T(8,128)(2,1)S(1)}, bf16[128,8192]{0,1:T(8,128)(2,1)}, u32[]{:S(2)}) copy-start(bf16[128,8192]{0,1:T(8,128)(2,1)} %copy.94) | copy-start | bytes 6291460
  207.3 4.4 %copy-start.9 = (bf16[512,16,128]{0,2,1:T(8,128)(2,1)S(1)}, bf16[512,16,128]{0,2,1:T(8,128)(2,1)}, u32[]{:S(2)}) copy-start(bf16[512,16,128]{0,2,1:T(8,128)(2,1)} %copy.88) | copy-start | bytes 6291460
  211.7 4.8 %copy-start.3 = (bf16[16,512,512]{2,1,0:T(8,128)(2,1)}, bf16[16,512,512]{2,1,0:T(8,128)(2,1)S(1)}, u32[]{:S(2)}) copy-start(bf16[16,512,512]{2,1,0:T(8,128)(2,1)S(1)} %select_convert_fusion) | copy-start | bytes 25165828
  211.7 4.8 %copy-start.5 = (bf16[512,16,128]{0,2,1:T(8,128)(2,1)S(1)}, bf16[512,16,128]{0,2,1:T(8,128)(2,1)}, u32[]{:S(2)}) copy-start(bf16[512,16,128]{0,2,1:T(8,128)(2,1)} %copy.103) | copy-start | bytes 6291460
  286.9 3.4 %copy-start.4 = (f32[16,128,512]{2,1,0:T(8,128)S(1)}, f32[16,128,512]{2,1,0:T(8,128)}, u32[]{:S(2)}) copy-start(f32[16,128,512]{2,1,0:T(8,128)} %fusion.50) | copy-start | bytes 12582916
  286.9 4.4 %copy-start.10 = (bf16[512,2048]{1,0:T(8,128)(2,1)S(1)}, bf16[512,2048]{1,0:T(8,128)(2,1)}, u32[]{:S(2)}) copy-start(bf16[512,2048]{1,0:T(8,128)(2,1)} %param.9) | copy-start | bytes 6291460
Sparse Core Ops, SparseCore 0:
  18.4 75.5 all-gather.4
  203.3 70.4 all-gather.6
where the time goes:
time: 318 us; the launch traced here: 316 us
  waiting for transfers between devices  122 us (38%)
  local copies, waits for them, and re-layouts  60.3 us (19%)
  matrix products  51.3 us (16%)
  other arithmetic  33.6 us (11%)
  blocking collectives  29.2 us (9%)
  between operations  14.2 us (4%)
  starting transfers between devices  4.72 us (1%)
    all_gather x1, waiting for transfers between devices, on_device(): lax.all_gather(local_state[None].astype(jnp.bfloat16), 'seq', axis=0, til...  63.4 us
    all_gather x1, waiting for transfers between devices, carried_in(): everything = lax.all_gather(value.astype(jnp.bfloat16), axis)  41.6 us
    unnamed x34, local copies, waits for them, and re-layouts  34.6 us
    all_to_all x1, blocking collectives, on_device(): lax.all_to_all(grad_rows, 'head', split_axis=1, concat_axis=0, tiled=True)  29.2 us
    all_to_all x1, waiting for transfers between devices, on_device(): lax.all_to_all(attn_out, 'head', split_axis=0, concat_axis=1, tiled=True)  17.4 us
    select_n x8, other arithmetic, step(): return jnp.where(reached, new, before)  12.9 us
    reshape x2, local copies, waits for them, and re-layouts, split_heads(): matrix.reshape(matrix.shape[0], matrix.shape[1] // head_dim, head_dim)  8.6 us
    dot_general x1, matrix products, on_device(): jnp.einsum('hts,thd->shd', grad_scores, queries, preferred_element_type=j...  7.93 us
  transfers between devices with their start and end apart: 3, of which 3 were waited for; matrix products, arithmetic and copies ran while one was open for 15% of the time, Pallas kernels for 0%

commit v1 on v0

--- a/solution.py
+++ b/solution.py
@@ -56,7 +56,10 @@
         "thd,hde->the", queries, prefix_low, preferred_element_type=jnp.float32
     )
     attn_out = attn_out.astype(jnp.bfloat16).reshape(tok_here, -1)
-    token_rows = lax.all_to_all(attn_out, "head", split_axis=0, concat_axis=1, tiled=True)
+    count = lax.axis_size("head")
+    shards = jnp.stack(jnp.split(attn_out, count, axis=0), axis=0)
+    shards = lax.all_to_all(shards, "head", split_axis=0, concat_axis=0)
+    token_rows = jnp.concatenate(shards, axis=1)
     rows_wide = token_rows.astype(jnp.float32)
     inv_rms = lax.rsqrt(jnp.mean(rows_wide * rows_wide, axis=1, keepdims=True) + 1e-06)
     normed = rows_wide * inv_rms

time: 318 us -> 300 us (0.943)
  blocking collectives: 29.2 us -> 56.3 us
  local copies, waits for them, and re-layouts: 60.3 us -> 39.1 us
  waiting for transfers between devices: 122 us -> 109 us
  starting transfers between devices: 4.72 us -> 0.08 us
  other arithmetic: 33.6 us -> 29 us
    all_to_all x0 -> x1, blocking collectives: none -> 28.2 us  [on_device(): shards = lax.all_to_all(shards, 'head', split_axis=0, concat_axis=0)]
    all_to_all x1 -> x0, waiting for transfers between devices: 17.4 us -> none  [on_device(): lax.all_to_all(attn_out, 'head', split_axis=0, concat_axis=1, tiled=True)]
    unnamed x34 -> x31, local copies, waits for them, and re-layouts: 34.6 us -> 23 us
    all_to_all x1 -> x0, starting transfers between devices: 4.46 us -> none  [on_device(): lax.all_to_all(attn_out, 'head', split_axis=0, concat_axis=1, tiled=True)]
    all_to_all x1 -> x0, local copies, waits for them, and re-layouts: 4.15 us -> none  [on_device(): lax.all_to_all(attn_out, 'head', split_axis=0, concat_axis=1, tiled=True)]
    all_gather x1, waiting for transfers between devices: 41.6 us -> 45.7 us  [carried_in(): everything = lax.all_gather(value.astype(jnp.bfloat16), axis)]
    all_to_all x1, local copies, waits for them, and re-layouts: 3.94 us -> 0.24 us  [on_device(): lax.all_to_all(grad_rows, 'head', split_axis=1, concat_axis=0, tiled=True)]
  transfers between devices with their start and end apart: 3 -> 2, of which waited for: 3 -> 2; matrix products, arithmetic and copies ran while one was open for 15% -> 11% of each run, Pallas kernels for 0% -> 0%
where the time goes in v1:
time: 300 us; the launch traced here: 299 us
  waiting for transfers between devices  109 us (36%)
  blocking collectives  56.3 us (19%)
  matrix products  51.8 us (17%)
  local copies, waits for them, and re-layouts  39.1 us (13%)
  other arithmetic  29 us (10%)
  between operations  14.2 us (5%)
    all_gather x1, waiting for transfers between devices, on_device(): lax.all_gather(local_state[None].astype(jnp.bfloat16), 'seq', axis=0, til...  62.8 us
    all_gather x1, waiting for transfers between devices, carried_in(): everything = lax.all_gather(value.astype(jnp.bfloat16), axis)  45.7 us
    all_to_all x1, blocking collectives, on_device(): shards = lax.all_to_all(shards, 'head', split_axis=0, concat_axis=0)  28.2 us
    all_to_all x1, blocking collectives, on_device(): lax.all_to_all(grad_rows, 'head', split_axis=1, concat_axis=0, tiled=True)  28.1 us
    unnamed x31, local copies, waits for them, and re-layouts  23 us
    select_n x8, other arithmetic, step(): return jnp.where(reached, new, before)  12.9 us
    reshape x2, local copies, waits for them, and re-layouts, split_heads(): matrix.reshape(matrix.shape[0], matrix.shape[1] // head_dim, head_dim)  8.61 us
    dot_general x1, matrix products, on_device(): jnp.einsum('hts,thd->shd', grad_scores, queries, preferred_element_type=j...  7.93 us
  transfers between devices with their start and end apart: 2, of which 2 were waited for; matrix products, arithmetic and copies ran while one was open for 11% of the time, Pallas kernels for 0%

profile of v1, /device:TPU:0, one launch (start us, length us, event | category | flops | bytes accessed | tf_op | source)
XLA Modules:
  0.0 299.3 jit_solution(2461580072358476877)
XLA Ops:
  7.2 3.7 %copy.86 = bf16[64,8,16,128]{3,2,1,0:T(8,128)(2,1)} copy(bf16[64,8,16,128]{3,1,2,0:T(8,128)(2,1)} %bitcast.131) | data formatting | bytes 4194304
  10.9 4.3 %copy.58 = bf16[512,16,128]{0,2,1:T(8,128)(2,1)} copy(bf16[512,16,128]{2,1,0:T(8,128)(2,1)} %bitcast.130) | data formatting | bytes 4194304 | tf_op jit(solution)/shard_map/reshape | solution.py:28
  15.2 3.1 %fusion.38 = bf16[16,128,128]{2,1,0:T(8,128)(2,1)} fusion(bf16[512,16,128]{0,2,1:T(8,128)(2,1)} %copy.58, bf16[512,2048]{1,0:T(8,128)(2,1)S(1)} %copy-done), kind=kOutput, calls=%fused_computation.53 | convolution fusion | flops 268697600 | bytes 4718592 | tf_op jit(solution)/shard_map/thd,the->hde/dot_general | solution.py:37
  18.5 4.6 %select_convert_fusion.1 = bf16[16,512,512]{2,1,0:T(8,128)(2,1)S(1)} fusion(pred[512,512]{1,0:T(8,128)(4,1)S(1)} %iota_compare_fusion, bf16[512,2048]{1,0:T(8,128)(2,1)} %param.9, bf16[512,2048]{1,0:T(8,128)(2,1)} %param.8), kind=kOutput, calls=%fused_computation.2 | convolution fusion | flops 1082130432 | bytes 12845056 | tf_op jit(solution)/shard_map/thd,shd->hts/dot_general | solution.py:49
  23.1 3.2 %copy-done.1 = bf16[16,512,512]{2,1,0:T(8,128)(2,1)} copy-done((bf16[16,512,512]{2,1,0:T(8,128)(2,1)}, bf16[16,512,512]{2,1,0:T(8,128)(2,1)S(1)}, u32[]{:S(2)}) %copy-start.1) | copy-done | bytes 8388632
  26.3 4.8 %fusion.11 = f32[16,512,128]{1,2,0:T(8,128)} fusion(bf16[16,512,512]{2,1,0:T(8,128)(2,1)S(1)} %select_convert_fusion.1, bf16[512,2048]{1,0:T(8,128)(2,1)S(1)} %copy-done), kind=kOutput, calls=%fused_computation.27 | convolution fusion | flops 1073741824 | bytes 14680064 | tf_op jit(solution)/shard_map/hts,she->the/dot_general | solution.py:52
  31.2 62.8 %all-gather.5.cloned.1.call-done = bf16[128,128,128]{2,1,0:T(8,128)(2,1)} async-done(((bf16[16,128,128]{2,1,0:T(8,128)(2,1)}), bf16[128,128,128]{2,1,0:T(8,128)(2,1)}) %all-gather.5.cloned.1.call-update) | async-done | bytes 4194320 | tf_op jit(solution)/shard_map/all_gather | solution.py:42
  94.0 3.3 %fusion = bf16[16,128,128]{2,1,0:T(8,128)(2,1)S(1)} fusion(bf16[8,16,128,128]{3,2,1,0:T(8,128)(2,1)} %bitcast.134, f32[8]{0:T(128)S(1)} %compare_convert_fusion), kind=kLoop, calls=%fused_computation.4 | loop fusion | flops 6029312 | bytes 4718624 | tf_op jit(solution)/shard_map/reduce_sum | solution.py:47
  97.4 2.6 fusion.10
  100.9 28.2 %all_to_all.21 = bf16[4,128,2048]{1,2,0:T(8,128)(2,1)S(1)} all-to-all(bf16[4,128,2048]{1,2,0:T(8,128)(2,1)S(1)} %pad_maximum_fusion), channel_id=1, replica_groups=mesh['seq'=8,'head'=4] {'head'}, dimensions={0} | all-to-all | bytes 4194304 | tf_op jit(solution)/shard_map/all_to_all | solution.py:61
  130.2 2.2 convert_element_type.94
  132.4 5.6 %copy.81 = f32[128,8192]{1,0:T(8,128)} copy(f32[128,8192]{0,1:T(8,128)} %bitcast.124) | data formatting | bytes 8388608 | tf_op jit(solution)/shard_map/convert_element_type | solution.py:63
  138.1 5.3 %multiply_reduce_fusion = f32[128]{0:T(128)S(1)} fusion(f32[128,8192]{1,0:T(8,128)} %copy.81, f32[128]{0:T(128)S(1)} %add_rsqrt_fusion, bf16[128,8192]{1,0:T(8,128)(2,1)} %param.11, f32[8192]{0:T(1024)S(1)} %copy-done.12, bf16[128,8192]{1,0:T(8,128)(2,1)} %param.13), kind=kLoop, calls=%fused_computation.23 | loop fusion | flops 11534208 | bytes 8422400 | tf_op jit(solution)/shard_map/reduce_sum | solution.py:73
  144.0 3.8 %fusion.7 = (bf16[128,8192]{1,0:T(8,128)(2,1)}, bf16[128,8192]{1,0:T(8,128)(2,1)S(1)}) fusion(bf16[128,8192]{1,0:T(8,128)(2,1)S(1)} %copy-done.7, bf16[128,8192]{1,0:T(8,128)(2,1)S(1)} %copy-done.8, f32[128,8192]{1,0:T(8,128)S(1)} %copy-done.2, f32[8192]{0:T(1024)S(1)} %copy-done.12, f32[128]{0:T(128)S(1)} %add_rsqrt_fusion, f32[128]{0:T(128)S(1)} %broadcast_multiply_fusion), kind=kLoop, calls=%fused_computation.14 | loop fusion | flops 20971520 | bytes 12616704 | tf_op jit(solution)/shard_map/convert_element_type | solution.py:69
  148.0 28.1 %all_to_all.22 = bf16[128,4,2048]{2,0,1:T(8,128)(2,1)S(1)} all-to-all(bf16[128,4,2048]{2,0,1:T(8,128)(2,1)S(1)} %bitcast.127), channel_id=1, replica_groups=mesh['seq'=8,'head'=4] {'head'}, dimensions={1} | all-to-all | bytes 4194304 | tf_op jit(solution)/shard_map/all_to_all | solution.py:75
  176.2 2.0 copy.87
  178.1 4.3 %copy.69 = bf16[512,16,128]{0,2,1:T(8,128)(2,1)} copy(bf16[512,16,128]{2,1,0:T(8,128)(2,1)} %bitcast.129) | data formatting | bytes 4194304 | tf_op jit(solution)/shard_map/reshape | solution.py:28
  182.5 2.9 fusion.41
  186.5 4.2 %select_convert_fusion = bf16[16,512,512]{2,1,0:T(8,128)(2,1)S(1)} fusion(bf16[512,16,128]{0,2,1:T(8,128)(2,1)} %copy.69, pred[512,512]{1,0:T(8,128)(4,1)S(1)} %iota_compare_fusion, bf16[512,2048]{1,0:T(8,128)(2,1)S(1)} %copy-done), kind=kOutput, calls=%fused_computation.1 | convolution fusion | flops 1082130432 | bytes 12845056 | tf_op jit(solution)/shard_map/the,she->hts/dot_general | solution.py:80
  190.8 4.8 %fusion.49 = f32[16,512,128]{1,2,0:T(8,128)} fusion(bf16[16,512,512]{2,1,0:T(8,128)(2,1)S(1)} %select_convert_fusion, bf16[512,16,128]{0,2,1:T(8,128)(2,1)S(1)} %copy-done.9), kind=kOutput, calls=%fused_computation.64 | convolution fusion | flops 1073741824 | bytes 14680064 | tf_op jit(solution)/shard_map/hts,shd->thd/dot_general | solution.py:84
  195.6 4.4 %fusion.9 = bf16[512,16,128]{0,2,1:T(8,128)(2,1)} fusion(f32[16,512,128]{1,2,0:T(8,128)} %fusion.49, bf16[512,16,128]{0,2,1:T(8,128)(2,1)S(1)} %copy-done.5, bf16[16,128,128]{2,1,0:T(8,128)(2,1)} %copy-done.11), kind=kOutput, calls=%fused_computation.18 | convolution fusion | flops 270532608 | bytes 8912896 | tf_op jit(solution)/shard_map/the,hde->thd/dot_general | solution.py:87
  200.1 3.9 %copy.76 = bf16[512,2048]{1,0:T(8,128)(2,1)} copy(bf16[512,2048]{0,1:T(8,128)(2,1)} %bitcast.126) | data formatting | bytes 4194304
  204.0 7.3 %fusion.50 = f32[16,128,512]{2,1,0:T(8,128)} fusion(bf16[512,16,128]{0,2,1:T(8,128)(2,1)} %copy.69, bf16[16,512,512]{2,1,0:T(8,128)(2,1)} %copy-done.1), kind=kOutput, calls=%fused_computation.65 | convolution fusion | flops 1073741824 | bytes 14680064 | tf_op jit(solution)/shard_map/hts,the->she/dot_general | solution.py:94
  211.3 45.7 %all-gather.7.cloned.1.call-done = bf16[128,128,128]{2,1,0:T(8,128)(2,1)} async-done(((bf16[16,128,128]{2,1,0:T(8,128)(2,1)}), bf16[128,128,128]{2,1,0:T(8,128)(2,1)}) %all-gather.7.cloned.1.call-update) | async-done | bytes 4194320 | tf_op jit(solution)/shard_map/all_gather | solution.py:11
  257.0 13.1 %while.16 = (s32[]{:T(128)}, f32[16,128,128]{2,1,0:T(8,128)S(1)}, s32[]{:T(128)}, bf16[8,16,128,128]{3,2,1,0:T(8,128)(2,1)}, s32[]{:T(128)}, /*index=5*/s32[]{:T(128)}, s32[]{:T(128)}, s32[]{:T(128)}) while((s32[]{:T(128)}, f32[16,128,128]{2,1,0:T(8,128)S(1)}, s32[]{:T(128)}, bf16[8,16,128,128]{3,2,1,0:T(8,128)(2,1)}, s32[]{:T(128)}, ...), condition=%wide.region_4.5_spmd.clone, body=%wide.region_3.4_spmd.clone.sunk | while | flops 1048584 | bytes 2621603 | solution.py:20
  258.7 1.6 add_select_fusion.2
  260.3 1.6 add_select_fusion.2
  270.2 2.9 fusion.13
  274.6 2.2 add_convert_fusion
  276.7 3.9 %copy.78 = bf16[512,2048]{1,0:T(8,128)(2,1)} copy(bf16[512,2048]{0,1:T(8,128)(2,1)} %bitcast.132) | data formatting | bytes 4194304
  280.6 7.9 %fusion.8 = bf16[512,16,128]{0,2,1:T(8,128)(2,1)} fusion(f32[16,128,512]{2,1,0:T(8,128)} %fusion.13, bf16[16,512,512]{2,1,0:T(8,128)(2,1)} %copy-done.3, bf16[512,2048]{1,0:T(8,128)(2,1)} %param.8), kind=kOutput, calls=%fused_computation.16 | convolution fusion | flops 1075838976 | bytes 16777216 | tf_op jit(solution)/shard_map/hts,thd->shd/dot_general | solution.py:90
  288.6 3.9 %copy.77 = bf16[512,2048]{1,0:T(8,128)(2,1)} copy(bf16[512,2048]{0,1:T(8,128)(2,1)} %bitcast.133) | data formatting | bytes 4194304
  (45 shorter events, 15.5 us)
Async XLA Ops:
  7.2 8.0 %copy-start = (bf16[512,2048]{1,0:T(8,128)(2,1)S(1)}, bf16[512,2048]{1,0:T(8,128)(2,1)}, u32[]{:S(2)}) copy-start(bf16[512,2048]{1,0:T(8,128)(2,1)} %param.10) | copy-start | bytes 6291460
  7.2 86.8 %all-gather.5.cloned.1.call-start = ((), (), s32[]{:S(2)}) async-start(), calls=%async_computation.2 | async-start | bytes 4718592 | tf_op jit(solution)/shard_map/all_gather | solution.py:42
  18.3 238.7 %all-gather.7.cloned.1.call-start = ((), (), s32[]{:S(2)}) async-start(), calls=%async_computation.3 | async-start | bytes 4718592 | tf_op jit(solution)/shard_map/all_gather | solution.py:11
  23.1 3.2 %copy-start.1 = (bf16[16,512,512]{2,1,0:T(8,128)(2,1)}, bf16[16,512,512]{2,1,0:T(8,128)(2,1)S(1)}, u32[]{:S(2)}) copy-start(bf16[16,512,512]{2,1,0:T(8,128)(2,1)S(1)} %select_convert_fusion.1) | copy-start | bytes 25165828
  94.0 3.4 %copy-start.6 = (f32[16,512,128]{1,2,0:T(8,128)S(1)}, f32[16,512,128]{1,2,0:T(8,128)}, u32[]{:S(2)}) copy-start(f32[16,512,128]{1,2,0:T(8,128)} %fusion.11) | copy-start | bytes 12582916
  97.4 2.6 copy-start.11
  132.4 5.6 %copy-start.12 = (f32[8192]{0:T(1024)S(1)}, f32[8192]{0:T(1024)}, u32[]{:S(2)}) copy-start(f32[8192]{0:T(1024)} %param.12) | copy-start | bytes 98308
  138.1 5.3 %copy-start.2 = (f32[128,8192]{1,0:T(8,128)S(1)}, f32[128,8192]{1,0:T(8,128)}, u32[]{:S(2)}) copy-start(f32[128,8192]{1,0:T(8,128)} %copy.81) | copy-start | bytes 12582916
  138.1 5.3 %copy-start.7 = (bf16[128,8192]{1,0:T(8,128)(2,1)S(1)}, bf16[128,8192]{1,0:T(8,128)(2,1)}, u32[]{:S(2)}) copy-start(bf16[128,8192]{1,0:T(8,128)(2,1)} %param.11) | copy-start | bytes 6291460
  138.1 5.9 %copy-start.8 = (bf16[128,8192]{1,0:T(8,128)(2,1)S(1)}, bf16[128,8192]{1,0:T(8,128)(2,1)}, u32[]{:S(2)}) copy-start(bf16[128,8192]{1,0:T(8,128)(2,1)} %param.13) | copy-start | bytes 6291460
  186.5 4.3 %copy-start.9 = (bf16[512,16,128]{0,2,1:T(8,128)(2,1)S(1)}, bf16[512,16,128]{0,2,1:T(8,128)(2,1)}, u32[]{:S(2)}) copy-start(bf16[512,16,128]{0,2,1:T(8,128)(2,1)} %copy.58) | copy-start | bytes 6291460
  190.7 4.9 %copy-start.3 = (bf16[16,512,512]{2,1,0:T(8,128)(2,1)}, bf16[16,512,512]{2,1,0:T(8,128)(2,1)S(1)}, u32[]{:S(2)}) copy-start(bf16[16,512,512]{2,1,0:T(8,128)(2,1)S(1)} %select_convert_fusion) | copy-start | bytes 25165828
  190.8 4.9 %copy-start.5 = (bf16[512,16,128]{0,2,1:T(8,128)(2,1)S(1)}, bf16[512,16,128]{0,2,1:T(8,128)(2,1)}, u32[]{:S(2)}) copy-start(bf16[512,16,128]{0,2,1:T(8,128)(2,1)} %copy.69) | copy-start | bytes 6291460
  270.2 3.4 %copy-start.4 = (f32[16,128,512]{2,1,0:T(8,128)S(1)}, f32[16,128,512]{2,1,0:T(8,128)}, u32[]{:S(2)}) copy-start(f32[16,128,512]{2,1,0:T(8,128)} %fusion.50) | copy-start | bytes 12582916
  270.2 4.4 %copy-start.10 = (bf16[512,2048]{1,0:T(8,128)(2,1)S(1)}, bf16[512,2048]{1,0:T(8,128)(2,1)}, u32[]{:S(2)}) copy-start(bf16[512,2048]{1,0:T(8,128)(2,1)} %param.9) | copy-start | bytes 6291460
Sparse Core Ops, SparseCore 0:
  18.4 75.5 all-gather.4
  186.6 70.4 all-gather.6
